TPU v7x, 32 devices: a whole 2x2x4 slice. The times are simulated.
32 devices in a mesh: tm: 4 (over x, core), tile: 8 (over z, y).
Axes of the slice: x: 2, y: 2, z: 4, core: 2. Of those that a mesh axis runs over, the one named last changes fastest.
Arguments:
- pcs: float32 [2, 256], P(None, 'tm'), may hold values from -6 to 6
- st_eof: float32 [2, 120, 512], replicated, may hold values from -6 to 6
- spatial_eof: bfloat16 [2, 512, 64, 2048], P(None, 'tm', 'tile'), may hold values from -1 to 1
- land_sea: int32 [64, 2048], P('tile'), may hold values 0 or 1
Outputs:
- vorticity: float32 [256, 64, 2048], P('tm', 'tile')
- divergence: float32 [256, 64, 2048], P('tm', 'tile')
All inputs are finite; a program needn't handle non-finite values. No bound on the sum of `land_sea` on one device may be relied on, other than what follows from the above.
Results may differ from a plain program's by a relative error of at most 0.0041.
Values may be sent and summed in bfloat16 or wider, within the bound.
A program may use at most 128 MiB of HBM per device.

v0:
```python
import math
import jax
import jax.numpy as jnp
from jax import lax
from jax.sharding import PartitionSpec as P


def padded_2(block, sides, width):
    for axis, dim in sides:
        count = lax.axis_size(axis)
        forward = [(i, i + 1) for i in range(count - 1)]
        backward = [(target, source) for source, target in forward]
        low = lax.ppermute(
            lax.slice_in_dim(block, block.shape[dim] - width, None, axis=dim), axis, forward
        )
        high = lax.ppermute(lax.slice_in_dim(block, 0, width, axis=dim), axis, backward)
        block = jnp.concatenate([low, block, high], axis=dim)
    return block


def lagged_rc(series, st_eof, first, count):
    day_index = first + jnp.arange(count, dtype=jnp.int32)
    lag_steps = jnp.arange(st_eof.shape[1], dtype=jnp.int32)
    lag_index = day_index[:, None] - lag_steps[None, :]
    inside = lag_index >= 0
    safe_index = jnp.maximum(lag_index, 0)
    values_lag = jnp.where(inside[None], series[:, safe_index], 0.0)
    lag_total = st_eof.shape[0] * st_eof.shape[1]
    lagged = jnp.transpose(values_lag, (1, 0, 2)).reshape(count, lag_total)
    lagged_sums = jnp.dot(
        lagged,
        st_eof.reshape(lag_total, -1),
        precision=lax.Precision.HIGHEST,
        preferred_element_type=jnp.float32,
    )
    window_len = jnp.minimum(day_index + 1, st_eof.shape[1]).astype(jnp.float32)
    return lagged_sums / window_len[:, None]


def curl_div(east_pad, north_pad, latitude):
    cosine = jnp.cos(latitude)
    cos_east = east_pad * cosine[None, :, None]
    cos_north = north_pad * cosine[None, :, None]
    inner_east = east_pad[:, 1:-1]
    inner_north = north_pad[:, 1:-1]
    zonal_east = jnp.roll(inner_east, -1, axis=2) - jnp.roll(inner_east, 1, axis=2)
    zonal_north = jnp.roll(inner_north, -1, axis=2) - jnp.roll(inner_north, 1, axis=2)
    denominator = 2.0 * cosine[1:-1][None, :, None]
    vorticity = (zonal_north - (cos_east[:, 2:] - cos_east[:, :-2])) / denominator
    divergence = (zonal_east + (cos_north[:, 2:] - cos_north[:, :-2])) / denominator
    return (vorticity, divergence)


def shards(pcs, st_eof, spatial_eof, land_sea):
    day_dev = pcs.shape[1]
    all_pcs = lax.all_gather(pcs, "tm", axis=1, tiled=True)
    own_index = lax.axis_index("tm")
    lat_rows, lon_cells = land_sea.shape
    cell_count = lat_rows * lon_cells
    chan_share = spatial_eof.shape[1]
    local_eof = spatial_eof.reshape(2, chan_share, cell_count)
    own_rc = lagged_rc(all_pcs, st_eof, own_index * day_dev, day_dev).astype(jnp.bfloat16)
    fields = jnp.einsum(
        "tc,xcn->txn",
        own_rc,
        lax.all_gather(local_eof, "tm", axis=1, tiled=True),
        preferred_element_type=jnp.float32,
    )
    ocean_mask = land_sea.astype(jnp.float32)
    velocity = (
        (fields * ocean_mask.reshape(1, 1, cell_count))
        .astype(jnp.bfloat16)
        .reshape(day_dev, 2, lat_rows, lon_cells)
    )
    padded = padded_2(velocity, (("tile", 2),), 1)
    total_rows = lat_rows * lax.axis_size("tile")
    global_rows = (lax.axis_index("tile") * lat_rows).astype(jnp.float32) + jnp.arange(
        -1, lat_rows + 1, dtype=jnp.float32
    )
    latitude = (-70.0 + 140.0 * (global_rows + 0.5) / total_rows) * (math.pi / 180.0)
    vorticity, divergence = curl_div(
        padded[:, 0].astype(jnp.float32), padded[:, 1].astype(jnp.float32), latitude
    )
    return (vorticity * ocean_mask[None], divergence * ocean_mask[None])


def solution(mesh):
    return jax.shard_map(
        shards,
        mesh=mesh,
        in_specs=(P(None, "tm"), P(), P(None, "tm", "tile", None), P("tile", None)),
        out_specs=(P("tm", "tile", None), P("tm", "tile", None)),
        check_vma=False,
    )
```

profile of v0, /device:TPU:0, one launch (start us, length us, event | category | flops | bytes accessed | tf_op | source)
XLA Modules:
  0.0 354.6 jit_solution(9750223347867482415)
XLA Ops:
  7.2 0.0 copy-start
  7.2 0.0 all-gather.3.cloned.1.call-start
  7.2 13.6 %reshape.93 = bf16[2,128,16384]{2,1,0:T(8,128)(2,1)} reshape(bf16[2,128,8,2048]{3,2,1,0:T(8,128)(2,1)} %param.6) | data formatting | bytes 16777216 | tf_op jit(solution)/shard_map/reshape | solution.py:61
  20.8 0.0 copy-start.4
  20.8 0.0 all-gather.3.cloned.1.call-update
  20.8 0.0 copy-start.3
  20.8 0.1 subtract_maximum_fusion
  20.9 0.1 reshape.99
  21.0 0.4 copy-done.4
  21.5 6.0 %all-gather = f32[4,64,2]{1,2,0:T(2,128)S(1)} all-gather(f32[1,64,2]{1,2,0:T(2,128)S(1)} %bitcast.56), channel_id=1, replica_groups=mesh['tm'=4,'tile'=8] {'tm'}, dimensions={0}, use_global_device_ids=true | all-gather | bytes 2560 | tf_op jit(solution)/shard_map/all_gather | solution.py:56
  27.5 0.1 copy.8
  27.6 14.9 %gather_fusion = f32[7680,2]{1,0:T(8,128)} fusion(f32[2,256]{0,1:T(8,128)S(1)} %bitcast.54, s32[8192]{0:T(1024)S(1)} %pad_clamp_fusion), kind=kCustom, calls=%fused_computation | custom fusion | bytes 153600 | tf_op jit(solution)/shard_map/gather | solution.py:27
  42.6 3.9 %copy.9 = f32[64,120,2]{1,0,2:T(8,128)S(1)} copy(f32[64,120,2]{2,1,0:T(8,128)} %bitcast.53) | data formatting | bytes 122880 | tf_op jit(solution)/shard_map/gather | solution.py:27
  46.4 0.0 copy-done.3
  46.5 0.1 subtract_compare_fusion
  46.6 0.0 copy-done
  46.6 0.4 fusion.11
  47.0 178.2 %all-gather.3.cloned.1.call-done = bf16[2,512,16384]{2,1,0:T(8,128)(2,1)} async-done(((bf16[2,128,16384]{2,1,0:T(8,128)(2,1)}), bf16[2,512,16384]{2,1,0:T(8,128)(2,1)}) %all-gather.3.cloned.1.call-update) | async-done | bytes 33554448 | tf_op jit(solution)/shard_map/all_gather | solution.py:66
  225.2 18.5 %fusion = bf16[64,2,16384]{2,0,1:T(8,128)(2,1)} fusion(bf16[64,512,1]{1,0,2:T(8,128)(2,1)S(1)} %fusion.11, bf16[2,512,16384]{2,1,0:T(8,128)(2,1)} %all-gather.3.cloned.1.call-done, f32[16384]{0:T(1024)S(1)} %bitcast.55), kind=kOutput, calls=%fused_computation.2 | convolution fusion | flops 2151677952 | bytes 37879808 | tf_op jit(solution)/shard_map/tc,xcn->txn/dot_general | solution.py:63
  243.7 5.0 %copy.17 = bf16[16,8,8,2048]{3,2,1,0:T(8,128)(2,1)S(1)} copy(bf16[16,8,8,2048]{3,1,2,0:T(8,128)(2,1)} %bitcast.50) | data formatting | bytes 8388608
  248.7 0.0 copy-start.2
  248.7 2.0 copy-done.2
  250.7 1.4 fusion.21
  252.1 0.3 copy.14
  252.4 3.4 collective-permute-start
  255.9 0.3 copy.15
  256.2 1.5 collective-permute-start.1
  257.7 0.1 multiply_cosine_fusion
  257.7 0.1 slice_multiply_fusion
  257.8 20.9 %collective-permute-done = bf16[64,2,1,2048]{3,0,2,1:T(8,128)(2,1)S(1)} collective-permute-done((bf16[64,2,1,2048]{3,0,2,1:T(8,128)(2,1)S(1)}, bf16[64,2,1,2048]{3,0,2,1:T(8,128)(2,1)S(1)}, u32[]{:S(2)}, u32[]{:S(2)}) %collective-permute-start) | collective-permute-done | bytes 524320 | tf_op jit(solution)/shard_map/ppermute | solution.py:13
  278.6 0.8 copy.12
  279.5 0.0 collective-permute-done.1
  279.5 0.8 copy.13
  280.3 8.5 %pad_maximum_fusion = bf16[64,2,10,2048]{3,2,0,1:T(8,128)(2,1)} fusion(bf16[64,2,1,2048]{3,2,0,1:T(2,128)(2,1)S(1)} %copy.13, bf16[64,2,8,2048]{3,2,0,1:T(8,128)(2,1)} %bitcast.52, bf16[64,2,1,2048]{3,2,0,1:T(2,128)(2,1)S(1)} %copy.12), kind=kLoop, calls=%fused_computation.3 | loop fusion | flops 15728640 | bytes 10485760 | tf_op jit(solution)/shard_map/concatenate | solution.py:17
  288.8 11.3 %fusion.7 = (f32[64,10,2048]{2,1,0:T(8,128)}, f32[64,10,2048]{2,1,0:T(8,128)}) fusion(bf16[64,2,10,2048]{3,2,0,1:T(8,128)(2,1)} %pad_maximum_fusion), kind=kLoop, calls=%fused_computation.13 | loop fusion | flops 2621440 | bytes 15728640 | tf_op jit(solution)/shard_map/convert_element_type | solution.py:82
  300.1 17.3 %fusion.18 = (f32[64,8,2047]{2,1,0:T(8,128)S(1)}, f32[64,8,2047]{2,1,0:T(8,128)}, f32[64,8,2047]{2,1,0:T(8,128)}, f32[64,8,2047]{2,1,0:T(8,128)}) fusion(f32[64,10,2048]{2,1,0:T(8,128)} %get-tuple-element.8, f32[64,10,2048]{2,1,0:T(8,128)} %get-tuple-element.9), kind=kLoop, calls=%fused_computation.38 | loop fusion | bytes 33538048 | tf_op jit(solution)/shard_map/jit(_roll_static)/slice | solution.py:46
  317.5 2.6 fusion.17
  320.1 9.3 %broadcast_multiply_fusion = (f32[64,10,2048]{2,1,0:T(8,128)}, f32[64,10,2048]{2,1,0:T(8,128)}) fusion(f32[10]{0:T(128)S(1)} %multiply_cosine_fusion, bf16[64,2,10,2048]{3,2,0,1:T(8,128)(2,1)} %pad_maximum_fusion), kind=kLoop, calls=%fused_computation.18 | loop fusion | flops 5242880 | bytes 15728680 | tf_op jit(solution)/shard_map/mul | solution.py:43
  329.4 0.0 copy-start.1
  329.4 18.3 %fusion.3 = (f32[64,8,2048]{2,1,0:T(8,128)}, f32[64,8,2048]{2,1,0:T(8,128)}) fusion(f32[64,10,2048]{2,1,0:T(8,128)} %get-tuple-element.2, f32[64,8,1]{2,1,0:T(8,128)} %get-tuple-element.5, f32[64,8,2047]{2,1,0:T(8,128)} %get-tuple-element.7, f32[64,8,2047]{2,1,0:T(8,128)S(1)} %get-tuple-element.6, f32[64,8,1]{2,1,0:T(8,128)S(1)} %get-tuple-element.4, ...), kind=kLoop, calls=%fused_computation.7 | loop fusion | flops 14680064 | bytes 42008608 | tf_op jit(solution)/shard_map/mul | solution.py:84
  347.7 0.0 copy-done.1
  (5 shorter events, 0.1 us)
Async XLA Ops:
  7.2 39.4 %copy-start = (f32[2,120,512]{2,1,0:T(8,128)S(1)}, f32[2,120,512]{2,1,0:T(8,128)}, u32[]{:S(2)}) copy-start(f32[2,120,512]{2,1,0:T(8,128)} %param.5) | copy-start | bytes 1474564
  7.2 218.0 %all-gather.3.cloned.1.call-start = ((), (), s32[]{:S(2)}) async-start(), calls=%async_computation | async-start | bytes 41943040 | tf_op jit(solution)/shard_map/all_gather | solution.py:66
  20.8 0.7 copy-start.4
  20.8 25.6 %copy-start.3 = (s32[8,2048]{1,0:T(8,128)S(1)}, s32[8,2048]{1,0:T(8,128)}, u32[]{:S(2)}) copy-start(s32[8,2048]{1,0:T(8,128)} %param.7) | copy-start | bytes 196612
  248.7 2.0 copy-start.2
  252.4 26.2 %collective-permute-start = (bf16[64,2,1,2048]{3,0,2,1:T(8,128)(2,1)S(1)}, bf16[64,2,1,2048]{3,0,2,1:T(8,128)(2,1)S(1)}, u32[]{:S(2)}, u32[]{:S(2)}) collective-permute-start(bf16[64,2,1,2048]{3,0,2,1:T(8,128)(2,1)S(1)} %copy.14), channel_id=1, source_target_pairs={{0,1},{1,2},{2,3},{3,4},{4,5},{5,6},{6,7},{8,9},{9,10},{10,11},{11... | collective-permute-start | bytes 1572872 | tf_op jit(solution)/shard_map/ppermute | solution.py:13
  256.2 23.3 %collective-permute-start.1 = (bf16[64,2,1,2048]{3,0,2,1:T(8,128)(2,1)S(1)}, bf16[64,2,1,2048]{3,0,2,1:T(8,128)(2,1)S(1)}, u32[]{:S(2)}, u32[]{:S(2)}) collective-permute-start(bf16[64,2,1,2048]{3,0,2,1:T(8,128)(2,1)S(1)} %copy.15), channel_id=1, source_target_pairs={{1,0},{2,1},{3,2},{4,3},{5,4},{6,5},{7,6},{9,8},{10,9},{11,10},{12... | collective-permute-start | bytes 1572872 | tf_op jit(solution)/shard_map/ppermute | solution.py:16
  329.4 18.3 %copy-start.1 = (f32[2,120,512]{2,1,0:T(8,128)S(1)}, f32[2,120,512]{2,1,0:T(8,128)}, u32[]{:S(2)}) copy-start(f32[2,120,512]{2,1,0:T(8,128)} %param.5) | copy-start | bytes 1474564
Sparse Core Ops, SparseCore 0:
  20.9 204.2 all-gather.2
where the time goes:
time: 355 us
  waiting for transfers between devices  199 us (56%)
  local copies, waits for them, and re-layouts  63.7 us (18%)
  other arithmetic  47.8 us (13%)
  matrix products  18.9 us (5%)
  between operations  14.2 us (4%)
  blocking collectives  6 us (2%)
  starting transfers between devices  4.92 us (1%)
    all_gather x1, waiting for transfers between devices, shards(): lax.all_gather(local_eof, 'tm', axis=1, tiled=True)  178 us
    ppermute x1, waiting for transfers between devices, padded_2(): lax.ppermute(lax.slice_in_dim(block, block.shape[dim] - width, None, axis...  20.9 us
    slice x2, local copies, waits for them, and re-layouts, curl_div(): jnp.roll(inner_east, 1, axis=2)  19.9 us
    gather x2, local copies, waits for them, and re-layouts, lagged_rc(): values_lag = jnp.where(inside[None], series[:, safe_index], 0.0)  18.8 us
    dot_general x1, matrix products, shards(): jnp.einsum('tc,xcn->txn', own_rc, lax.all_gather(local_eof, 'tm', axis=1,...  18.5 us
    mul x1, other arithmetic, shards(): return (vorticity * ocean_mask[None], divergence * ocean_mask[None])  18.3 us
    reshape x1, local copies, waits for them, and re-layouts, shards(): local_eof = spatial_eof.reshape(2, chan_share, cell_count)  13.6 us
    convert_element_type x1, other arithmetic, shards(): padded[:, 0].astype(jnp.float32)  11.3 us
  transfers between devices with their start and end apart: 3, of which 2 were waited for; matrix products, arithmetic and copies ran while one was open for 6% of the time, Pallas kernels for 0%

commit v1 on v0

--- a/solution.py
+++ b/solution.py
@@ -3,6 +3,29 @@
 import jax.numpy as jnp
 from jax import lax
 from jax.sharding import PartitionSpec as P
+
+
+def joined_along(tiles, dim):
+    tiles = jnp.moveaxis(tiles, 0, dim)
+    shape = tiles.shape
+    return tiles.reshape(*shape[:dim], shape[dim] * shape[dim + 1], *shape[dim + 2 :])
+
+
+def grow_blocks(x, axis):
+    size, place = (lax.axis_size(axis), lax.axis_index(axis))
+    blocks, stride = (x[None], 1)
+    while stride < size:
+        partner_block = lax.ppermute(blocks, axis, [(i, i ^ stride) for i in range(size)])
+        low = place & stride == 0
+        blocks = jnp.concatenate(
+            [jnp.where(low, blocks, partner_block), jnp.where(low, partner_block, blocks)]
+        )
+        stride *= 2
+    return blocks
+
+
+def gather_by_bits(x, axis, dim):
+    return joined_along(grow_blocks(x, axis), dim)
 
 
 def padded_2(block, sides, width):
@@ -63,7 +86,7 @@
     fields = jnp.einsum(
         "tc,xcn->txn",
         own_rc,
-        lax.all_gather(local_eof, "tm", axis=1, tiled=True),
+        gather_by_bits(local_eof, "tm", 1),
         preferred_element_type=jnp.float32,
     )
     ocean_mask = land_sea.astype(jnp.float32)

time: 355 us -> 602 us (1.70)
  blocking collectives: 6 us -> 361 us
  waiting for transfers between devices: 199 us -> 34.1 us
  other arithmetic: 47.8 us -> 109 us
  between operations: 14.2 us -> 1 us
    all_gather x1, blocking collectives: 6 us -> 361 us  [shards(): all_pcs = lax.all_gather(pcs, 'tm', axis=1, tiled=True)]
    all_gather x1 -> x0, waiting for transfers between devices: 178 us -> none  [shards(): lax.all_gather(local_eof, 'tm', axis=1, tiled=True)]
    concatenate x0 -> x2, other arithmetic: none -> 32 us  [grow_blocks(): jnp.concatenate([jnp.where(low, blocks, partner_block), jnp.where(low, pa...]
    select_n x0 -> x2, other arithmetic: none -> 28.9 us  [grow_blocks(): jnp.where(low, blocks, partner_block)]
    reshape x1 -> x0, local copies, waits for them, and re-layouts: 13.6 us -> none  [shards(): local_eof = spatial_eof.reshape(2, chan_share, cell_count)]
    another operation x0 -> x1, local copies, waits for them, and re-layouts: none -> 13.5 us  [grow_blocks(): blocks, stride = (x[None], 1)]
    ppermute x0 -> x2, waiting for transfers between devices: none -> 13.1 us  [grow_blocks(): lax.ppermute(blocks, axis, [(i, i ^ stride) for i in range(size)])]
    slice x0 -> x2, local copies, waits for them, and re-layouts: none -> 11.4 us  [curl_div(): jnp.roll(inner_north, 1, axis=2)]
  transfers between devices with their start and end apart: 3 -> 4, of which waited for: 2 -> 2; matrix products, arithmetic and copies ran while one was open for 6% -> 3% of each run, Pallas kernels for 0% -> 0%
where the time goes in v1:
time: 602 us; the launch traced here: 601 us
  blocking collectives  361 us (60%)
  other arithmetic  109 us (18%)
  local copies, waits for them, and re-layouts  67.9 us (11%)
  waiting for transfers between devices  34.1 us (6%)
  matrix products  18.9 us (3%)
  starting transfers between devices  8.52 us (1%)
    all_gather x1, blocking collectives, shards(): all_pcs = lax.all_gather(pcs, 'tm', axis=1, tiled=True)  361 us
    concatenate x2, other arithmetic, grow_blocks(): jnp.concatenate([jnp.where(low, blocks, partner_block), jnp.where(low, pa...  32 us
    select_n x2, other arithmetic, grow_blocks(): jnp.where(low, blocks, partner_block)  28.9 us
    ppermute x1, waiting for transfers between devices, padded_2(): lax.ppermute(lax.slice_in_dim(block, block.shape[dim] - width, None, axis...  21 us
    dot_general x1, matrix products, shards(): jnp.einsum('tc,xcn->txn', own_rc, gather_by_bits(local_eof, 'tm', 1), pre...  18.5 us
    mul x1, other arithmetic, shards(): return (vorticity * ocean_mask[None], divergence * ocean_mask[None])  18.3 us
    gather x2, local copies, waits for them, and re-layouts, lagged_rc(): values_lag = jnp.where(inside[None], series[:, safe_index], 0.0)  17.6 us
    another operation x1, local copies, waits for them, and re-layouts, grow_blocks(): blocks, stride = (x[None], 1)  13.5 us
  transfers between devices with their start and end apart: 4, of which 2 were waited for; matrix products, arithmetic and copies ran while one was open for 3% of the time, Pallas kernels for 0%

profile of v1, /device:TPU:0, one launch (start us, length us, event | category | flops | bytes accessed | tf_op | source)
XLA Modules:
  0.0 600.9 jit_solution(10615774104513090774)
XLA Ops:
  0.6 0.0 copy-start
  0.6 13.5 %broadcast_in_dim_reshape.3 = bf16[1,2,128,16384]{3,2,1,0:T(8,128)(2,1)} reshape(bf16[2,128,8,2048]{3,2,1,0:T(8,128)(2,1)} %param.6) | data formatting | bytes 16777216 | tf_op jit(solution)/shard_map/broadcast_in_dim;reshape | solution.py:16
  14.2 0.5 collective-permute-start
  14.7 13.1 %collective-permute-done = bf16[1,2,128,16384]{3,2,0,1:T(8,128)(2,1)} collective-permute-done((bf16[1,2,128,16384]{3,2,0,1:T(8,128)(2,1)}, bf16[1,2,128,16384]{3,2,0,1:T(8,128)(2,1)}, u32[]{:S(2)}, u32[]{:S(2)}) %collective-permute-start) | collective-permute-done | bytes 8388640 | tf_op jit(solution)/shard_map/ppermute | solution.py:18
  27.8 6.5 %broadcast_select_fusion.3 = (bf16[1,2,128,16384]{3,2,0,1:T(8,128)(2,1)S(1)}, bf16[1,2,128,16384]{3,2,0,1:T(8,128)(2,1)S(1)}) fusion(bf16[1,2,128,16384]{3,2,0,1:T(8,128)(2,1)} %collective-permute-done, pred[]{:T(512)S(6)} %eq.7, bf16[1,2,128,16384]{3,2,1,0:T(8,128)(2,1)} %broadcast_in_dim_reshape.3), kind=kLoop, calls=%fused_computation.9 | loop fusion | flops 8388608 | bytes 33554432 | tf_op jit(solution)/shard_map/jit(_where)/select_n | solution.py:21
  34.3 0.0 copy-start.2
  34.3 0.0 copy-start.3
  34.3 0.0 copy-start.6
  34.3 0.0 copy-start.5
  34.3 9.1 %pad_maximum_fusion.1 = bf16[2,2,128,16384]{3,2,0,1:T(8,128)(2,1)} fusion(bf16[1,2,128,16384]{3,2,0,1:T(8,128)(2,1)S(1)} %get-tuple-element.5, bf16[1,2,128,16384]{3,2,0,1:T(8,128)(2,1)S(1)} %get-tuple-element.4), kind=kLoop, calls=%fused_computation.4 | loop fusion | flops 8388608 | bytes 33554432 | tf_op jit(solution)/shard_map/concatenate | solution.py:20
  43.4 0.0 copy-done.2
  43.4 1.6 copy-done.3
  45.1 2.8 collective-permute-start.1
  47.9 0.1 subtract_maximum_fusion
  48.0 0.1 reshape.99
  48.1 0.0 copy-done.6
  48.1 361.5 %all-gather = f32[4,64,2]{1,2,0:T(2,128)S(1)} all-gather(f32[1,64,2]{1,2,0:T(2,128)S(1)} %bitcast.66), channel_id=1, replica_groups=mesh['tm'=4,'tile'=8] {'tm'}, dimensions={0}, use_global_device_ids=true | all-gather | bytes 2560 | tf_op jit(solution)/shard_map/all_gather | solution.py:79
  409.6 0.1 copy.14
  409.7 14.9 %gather_fusion = f32[7680,2]{1,0:T(8,128)} fusion(f32[2,256]{0,1:T(8,128)S(1)} %bitcast.64, s32[8192]{0:T(1024)S(1)} %pad_clamp_fusion), kind=kCustom, calls=%fused_computation | custom fusion | bytes 153600 | tf_op jit(solution)/shard_map/gather | solution.py:50
  424.7 2.7 copy.15
  427.4 0.0 copy-done.5
  427.4 0.1 subtract_compare_fusion
  427.5 0.0 copy-done
  427.5 0.4 fusion.11
  427.9 0.0 collective-permute-done.1
  428.0 22.4 %broadcast_select_fusion.1 = (bf16[2,2,128,16384]{3,2,0,1:T(8,128)(2,1)}, bf16[2,2,128,16384]{3,2,0,1:T(8,128)(2,1)}) fusion(bf16[2,2,128,16384]{3,2,0,1:T(8,128)(2,1)} %collective-permute-done.1, pred[]{:T(512)S(6)} %eq.6, bf16[1,2,128,16384]{3,2,0,1:T(8,128)(2,1)} %copy-done.3, bf16[1,2,128,16384]{3,2,0,1:T(8,128)(2,1)} %copy-done.2), kind=kLoop, calls=%fused_computation.6 | loop fusion | flops 25165824 | bytes 67108864 | tf_op jit(solution)/shard_map/jit(_where)/select_n | solution.py:21
  450.4 22.9 %pad_maximum_fusion = bf16[4,2,128,16384]{3,2,0,1:T(8,128)(2,1)} fusion(bf16[2,2,128,16384]{3,2,0,1:T(8,128)(2,1)} %get-tuple-element.3, bf16[2,2,128,16384]{3,2,0,1:T(8,128)(2,1)} %get-tuple-element.2), kind=kLoop, calls=%fused_computation.1 | loop fusion | flops 16777216 | bytes 67108864 | tf_op jit(solution)/shard_map/concatenate | solution.py:20
  473.3 18.5 %fusion = bf16[64,2,16384]{2,0,1:T(8,128)(2,1)} fusion(bf16[64,512,1]{1,0,2:T(8,128)(2,1)S(1)} %fusion.11, bf16[2,512,16384]{2,1,0:T(8,128)(2,1)} %bitcast.58, f32[16384]{0:T(1024)S(1)} %bitcast.65), kind=kOutput, calls=%fused_computation.3 | convolution fusion | flops 2151677952 | bytes 37879808 | tf_op jit(solution)/shard_map/tc,xcn->txn/dot_general | solution.py:86
  491.8 5.0 copy.26
  496.8 0.0 copy-start.4
  496.8 2.0 copy-done.4
  498.8 1.4 fusion.21
  500.3 0.3 copy.23
  500.6 3.7 collective-permute-start.2
  504.3 0.3 copy.24
  504.6 1.5 collective-permute-start.3
  506.1 0.1 multiply_cosine_fusion
  506.1 0.1 slice_multiply_fusion
  506.2 21.0 %collective-permute-done.2 = bf16[64,2,1,2048]{3,0,2,1:T(8,128)(2,1)S(1)} collective-permute-done((bf16[64,2,1,2048]{3,0,2,1:T(8,128)(2,1)S(1)}, bf16[64,2,1,2048]{3,0,2,1:T(8,128)(2,1)S(1)}, u32[]{:S(2)}, u32[]{:S(2)}) %collective-permute-start.2) | collective-permute-done | bytes 524320 | tf_op jit(solution)/shard_map/ppermute | solution.py:36
  527.2 0.8 copy.21
  528.0 0.0 collective-permute-done.3
  528.0 0.8 copy.22
  528.8 8.5 %pad_maximum_fusion.2 = bf16[64,2,10,2048]{3,2,0,1:T(8,128)(2,1)} fusion(bf16[64,2,1,2048]{3,2,0,1:T(2,128)(2,1)S(1)} %copy.22, bf16[64,2,8,2048]{3,2,0,1:T(8,128)(2,1)} %bitcast.62, bf16[64,2,1,2048]{3,2,0,1:T(2,128)(2,1)S(1)} %copy.21), kind=kLoop, calls=%fused_computation.7 | loop fusion | flops 15728640 | bytes 10485760 | tf_op jit(solution)/shard_map/concatenate | solution.py:40
  537.3 11.4 %fusion.7 = (f32[64,10,2048]{2,1,0:T(8,128)}, f32[64,10,2048]{2,1,0:T(8,128)}) fusion(bf16[64,2,10,2048]{3,2,0,1:T(8,128)(2,1)} %pad_maximum_fusion.2), kind=kLoop, calls=%fused_computation.19 | loop fusion | flops 2621440 | bytes 15728640 | tf_op jit(solution)/shard_map/convert_element_type | solution.py:105
  548.7 9.3 %fusion.20 = (f32[64,8,2047]{2,1,0:T(8,128)S(1)}, f32[64,8,2047]{2,1,0:T(8,128)}) fusion(f32[64,10,2048]{2,1,0:T(8,128)} %get-tuple-element.13), kind=kLoop, calls=%fused_computation.46 | loop fusion | bytes 16769024 | tf_op jit(solution)/shard_map/jit(_roll_static)/slice | solution.py:70
  558.0 2.0 fusion.19
  560.1 10.7 %fusion.18 = (f32[64,8,2047]{2,1,0:T(8,128)}, f32[64,8,2047]{2,1,0:T(8,128)}) fusion(f32[64,10,2048]{2,1,0:T(8,128)} %get-tuple-element.12), kind=kLoop, calls=%fused_computation.44 | loop fusion | bytes 16769024 | tf_op jit(solution)/shard_map/jit(_roll_static)/slice | solution.py:69
  570.7 2.1 fusion.17
  572.9 9.5 %broadcast_multiply_fusion = (f32[64,10,2048]{2,1,0:T(8,128)}, f32[64,10,2048]{2,1,0:T(8,128)}) fusion(f32[10]{0:T(128)S(1)} %multiply_cosine_fusion, bf16[64,2,10,2048]{3,2,0,1:T(8,128)(2,1)} %pad_maximum_fusion.2), kind=kLoop, calls=%fused_computation.24 | loop fusion | flops 5242880 | bytes 15728680 | tf_op jit(solution)/shard_map/mul | solution.py:66
  582.3 0.0 copy-start.1
  582.3 18.3 %fusion.3 = (f32[64,8,2048]{2,1,0:T(8,128)}, f32[64,8,2048]{2,1,0:T(8,128)}) fusion(f32[64,10,2048]{2,1,0:T(8,128)} %get-tuple-element.6, f32[64,8,1]{2,1,0:T(8,128)} %get-tuple-element.9, f32[64,8,2047]{2,1,0:T(8,128)} %get-tuple-element.11, f32[64,8,2047]{2,1,0:T(8,128)} %get-tuple-element.10, f32[64,8,1]{2,1,0:T(8,128)} %get-tuple-element.8, ...), kind=kLoop, calls=%fused_computation.13 | loop fusion | flops 14680064 | bytes 42008608 | tf_op jit(solution)/shard_map/mul | solution.py:107
  600.7 0.0 copy-done.1
  (4 shorter events, 0.1 us)
Async XLA Ops:
  0.6 426.9 %copy-start = (f32[2,120,512]{2,1,0:T(8,128)S(1)}, f32[2,120,512]{2,1,0:T(8,128)}, u32[]{:S(2)}) copy-start(f32[2,120,512]{2,1,0:T(8,128)} %param.5) | copy-start | bytes 1474564
  14.2 13.6 %collective-permute-start = (bf16[1,2,128,16384]{3,2,0,1:T(8,128)(2,1)}, bf16[1,2,128,16384]{3,2,0,1:T(8,128)(2,1)}, u32[]{:S(2)}, u32[]{:S(2)}) collective-permute-start(bf16[1,2,128,16384]{3,2,0,1:T(8,128)(2,1)} %bitcast.59), channel_id=1, source_target_pairs={{0,8},{8,0},{16,24},{24,16},{1,9},{9,1},{17,25},{25,17},{2,10},{10... | collective-permute-start | bytes 25165832 | tf_op jit(solution)/shard_map/ppermute | solution.py:18
  34.3 9.1 %copy-start.2 = (bf16[1,2,128,16384]{3,2,0,1:T(8,128)(2,1)}, bf16[1,2,128,16384]{3,2,0,1:T(8,128)(2,1)S(1)}, u32[]{:S(2)}) copy-start(bf16[1,2,128,16384]{3,2,0,1:T(8,128)(2,1)S(1)} %get-tuple-element.4) | copy-start | bytes 25165828
  34.3 10.8 %copy-start.3 = (bf16[1,2,128,16384]{3,2,0,1:T(8,128)(2,1)}, bf16[1,2,128,16384]{3,2,0,1:T(8,128)(2,1)S(1)}, u32[]{:S(2)}) copy-start(bf16[1,2,128,16384]{3,2,0,1:T(8,128)(2,1)S(1)} %get-tuple-element.5) | copy-start | bytes 25165828
  34.3 13.8 %copy-start.6 = (f32[2,64]{1,0:T(2,128)S(1)}, f32[2,64]{1,0:T(2,128)}, u32[]{:S(2)}) copy-start(f32[2,64]{1,0:T(2,128)} %param.4) | copy-start | bytes 1540
  34.3 393.0 %copy-start.5 = (s32[8,2048]{1,0:T(8,128)S(1)}, s32[8,2048]{1,0:T(8,128)}, u32[]{:S(2)}) copy-start(s32[8,2048]{1,0:T(8,128)} %param.7) | copy-start | bytes 196612
  45.1 382.9 %collective-permute-start.1 = (bf16[2,2,128,16384]{3,2,0,1:T(8,128)(2,1)}, bf16[2,2,128,16384]{3,2,0,1:T(8,128)(2,1)}, u32[]{:S(2)}, u32[]{:S(2)}) collective-permute-start(bf16[2,2,128,16384]{3,2,0,1:T(8,128)(2,1)} %pad_maximum_fusion.1), channel_id=1, source_target_pairs={{0,16},{8,24},{16,0},{24,8},{1,17},{9,25},{17,1},{25,9},{2,18},{10... | collective-permute-start | bytes 50331656 | tf_op jit(solution)/shard_map/ppermute | solution.py:18
  496.8 2.0 copy-start.4
  500.6 26.6 %collective-permute-start.2 = (bf16[64,2,1,2048]{3,0,2,1:T(8,128)(2,1)S(1)}, bf16[64,2,1,2048]{3,0,2,1:T(8,128)(2,1)S(1)}, u32[]{:S(2)}, u32[]{:S(2)}) collective-permute-start(bf16[64,2,1,2048]{3,0,2,1:T(8,128)(2,1)S(1)} %copy.23), channel_id=1, source_target_pairs={{0,1},{1,2},{2,3},{3,4},{4,5},{5,6},{6,7},{8,9},{9,10},{10,11},{11... | collective-permute-start | bytes 1572872 | tf_op jit(solution)/shard_map/ppermute | solution.py:36
  504.6 23.4 %collective-permute-start.3 = (bf16[64,2,1,2048]{3,0,2,1:T(8,128)(2,1)S(1)}, bf16[64,2,1,2048]{3,0,2,1:T(8,128)(2,1)S(1)}, u32[]{:S(2)}, u32[]{:S(2)}) collective-permute-start(bf16[64,2,1,2048]{3,0,2,1:T(8,128)(2,1)S(1)} %copy.24), channel_id=1, source_target_pairs={{1,0},{2,1},{3,2},{4,3},{5,4},{6,5},{7,6},{9,8},{10,9},{11,10},{12... | collective-permute-start | bytes 1572872 | tf_op jit(solution)/shard_map/ppermute | solution.py:39
  582.3 18.4 %copy-start.1 = (f32[2,120,512]{2,1,0:T(8,128)S(1)}, f32[2,120,512]{2,1,0:T(8,128)}, u32[]{:S(2)}) copy-start(f32[2,120,512]{2,1,0:T(8,128)} %param.5) | copy-start | bytes 1474564
